TPU v7x, 128 devices: a whole 4x4x4 slice. The times are simulated.
128 devices in a mesh: pix: 64 (over x, z, y_hi, core), col: 2 (over y_lo).
Axes of the slice: x: 4, y: 4 (y_hi: 2, y_lo: 2; y = y_hi * 2 + y_lo), z: 4, core: 2. Of those that a mesh axis runs over, the one named last changes fastest.
Arguments:
- observed: float32 [16384, 4096], P('pix', 'col'), may hold values from -40 to 40
- valid_mask: int32 [16384, 512], P('pix', 'col'), may hold values 0 or 1
- pix_factor: float32 [16384, 256], P('pix'), may hold values from -6 to 6
- col_factor: float32 [4096, 256], P('col'), may hold values from -0.375 to 0.375
Outputs:
- pix_next: float32 [16384, 256], P('pix')
- col_next: float32 [4096, 256], P('col')
- cloud: float32 [16384, 4096], P('pix', 'col')
All inputs are finite; a program needn't handle non-finite values. No bound on the sum of `valid_mask` on one device may be relied on, other than what follows from the above.
Results may differ from a plain program's by a relative error of at most 0.0003.
Values sent between devices are 32-bit elements; how exact they have to be, the bound alone decides.
A program may use at most 64 MiB of HBM per device.

v0:
```python
import jax
import jax.numpy as jnp
from jax import lax
from jax.sharding import PartitionSpec as P

BANDS = 8
WIDTH = 256
ITERS = 2
PASSES = 2
highest = lax.Precision.HIGHEST
threshold_scale = 1.0
diffusion = 0.2


def passed_along(block, axis, distance):
    devices = range(lax.axis_size(axis))
    route = [(i - distance, i) for i in devices if i - distance in devices]
    return lax.ppermute(block, axis, route)


def soft_cut(values, level):
    return jnp.sign(values) * jnp.maximum(jnp.abs(values) - level, 0.0)


def flux_of(diff, level):
    return diff / (1.0 + (diff / level) ** 2)


def level_of(residual, weight, total):
    spread = lax.psum(jnp.sum(weight * residual * residual), ("pix", "col"))
    return threshold_scale * jnp.sqrt(spread / total + 1e-06)


def smooth_pass(grid, level, strip_index, pix_count):
    has_north = strip_index > 0
    has_south = strip_index < pix_count - 1
    top_row = grid[0]
    bottom_row = grid[-1]
    north_rim = passed_along(bottom_row, "pix", 1)
    south_rim = passed_along(top_row, "pix", -1)
    north_rim = jnp.where(has_north, north_rim, top_row)
    south_rim = jnp.where(has_south, south_rim, bottom_row)
    north = jnp.concatenate([north_rim[None], grid[:-1]], axis=0)
    south = jnp.concatenate([grid[1:], south_rim[None]], axis=0)
    west = jnp.concatenate([grid[:, :1], grid[:, :-1]], axis=1)
    east = jnp.concatenate([grid[:, 1:], grid[:, -1:]], axis=1)
    summed = flux_of(north - grid, level) + flux_of(south - grid, level)
    summed = summed + flux_of(west - grid, level) + flux_of(east - grid, level)
    return grid + diffusion * summed


def per_device(observed, valid_mask, pix_factor, col_factor):
    pix_count = lax.axis_size("pix")
    col_count = lax.axis_size("col")
    pixels, columns = observed.shape
    dates = valid_mask.shape[1]
    weight = jnp.broadcast_to(
        valid_mask.astype(jnp.float32)[:, :, None], (pixels, dates, BANDS)
    ).reshape(pixels, columns)
    total = float(pixels * columns * pix_count * col_count)
    pix_fac = pix_factor
    col_fac = col_factor
    low_rank = jnp.dot(pix_fac, col_fac.T, precision=highest)
    for iteration in range(ITERS):
        residual = observed - low_rank
        level = level_of(residual, weight, total)
        sparse = weight * soft_cut(residual, level)
        misfit = weight * (sparse - residual)
        pix_grad = lax.psum(jnp.dot(misfit, col_fac, precision=highest), "col")
        change = jnp.dot(pix_grad, col_fac.T, precision=highest)
        norm_local = jnp.sum(pix_grad * pix_grad)
        curve_local = jnp.sum(weight * change * change)
        top_sum = lax.psum(norm_local, "pix")
        bottom_sum = lax.psum(curve_local, ("pix", "col"))
        step_pix = top_sum / bottom_sum
        pix_fac = pix_fac - step_pix * pix_grad
        low_rank = low_rank - step_pix * change
        misfit = weight * (sparse - (observed - low_rank))
        local_grad = lax.dot_general(
            misfit,
            pix_fac,
            (((0,), (0,)), ((), ())),
            precision=highest,
            preferred_element_type=jnp.float32,
        )
        col_grad = lax.psum(local_grad, "pix")
        shifted = jnp.dot(pix_fac, col_grad.T, precision=highest)
        norm_local = jnp.sum(col_grad * col_grad)
        curve_local = jnp.sum(weight * shifted * shifted)
        top_sum = lax.psum(norm_local, "col")
        bottom_sum = lax.psum(curve_local, ("pix", "col"))
        step_col = top_sum / bottom_sum
        col_fac = col_fac - step_col * col_grad
        low_rank = low_rank - step_col * shifted
    residual = observed - low_rank
    level = level_of(residual, weight, total)
    layer = weight * soft_cut(residual, level)
    strip_index = lax.axis_index("pix")
    grid = layer.reshape(pixels // WIDTH, WIDTH, columns)
    for sweep_index in range(PASSES):
        grid = smooth_pass(grid, level, strip_index, pix_count)
    return (pix_fac, col_fac, grid.reshape(pixels, columns))


def solution(mesh):
    in_specs = (P("pix", "col"), P("pix", "col"), P("pix", None), P("col", None))
    out_specs = (P("pix", None), P("col", None), P("pix", "col"))
    return jax.shard_map(
        per_device, mesh=mesh, in_specs=in_specs, out_specs=out_specs, check_vma=False
    )
```

profile of v0, /device:TPU:32, one launch (start us, length us, event | category | flops | bytes accessed | tf_op | source)
XLA Modules:
  0.0 2382.3 jit_solution(10405248718728174888)
XLA Ops:
  7.2 0.0 all-reduce.5.cloned.1.call-start
  7.2 1.0 convert_element_type.3
  8.2 0.1 copy.7
  8.3 1.5 broadcast_bitcast_fusion
  9.8 2.0 copy.10
  11.8 7.0 fusion
  18.7 65.8 %psum.105 = f32[]{:T(128)} all-reduce(f32[]{:T(128)} %get-tuple-element.8), channel_id=1, replica_groups=mesh['pix'=64,'col'=2] {'pix','col'}, use_global_device_ids=true, to_apply=%region_1.0 | all-reduce | flops 1 | bytes 8 | tf_op jit(solution)/shard_map/psum | solution.py:30
  85.2 5.7 fusion.20
  91.0 0.0 all-reduce.5.cloned.1.call-update
  91.0 0.0 all-reduce.7.cloned.1.call-start
  91.0 28.1 %all-reduce.5.cloned.1.call-done = f32[256,256]{1,0:T(8,128)} async-done(((f32[256,256]{1,0:T(8,128)}), f32[256,256]{1,0:T(8,128)}) %all-reduce.5.cloned.1.call-update) | async-done | bytes 262160 | tf_op jit(solution)/shard_map/psum | solution.py:69
  119.1 1.6 multiply_reduce_fusion.3
  120.7 156.7 %psum.107 = f32[]{:T(128)} all-reduce(f32[]{:T(128)} %multiply_reduce_fusion.3), channel_id=1, replica_groups=mesh['pix'=64,'col'=2] {'pix'}, use_global_device_ids=true, to_apply=%region_4.0 | all-reduce | flops 1 | bytes 8 | tf_op jit(solution)/shard_map/psum | solution.py:73
  277.5 5.6 fusion.1
  283.1 72.4 %psum.108 = f32[]{:T(128)} all-reduce(f32[]{:T(128)} %get-tuple-element.19), channel_id=1, replica_groups=mesh['pix'=64,'col'=2] {'pix','col'}, use_global_device_ids=true, to_apply=%region_6.0 | all-reduce | flops 1 | bytes 8 | tf_op jit(solution)/shard_map/psum | solution.py:74
  356.8 0.0 copy-done.6
  356.8 9.0 fusion.16
  365.8 0.0 all-reduce.7.cloned.1.call-update
  365.8 0.0 all-reduce.9.cloned.1.call-start
  365.9 638.4 %all-reduce.7.cloned.1.call-done = f32[2048,256]{1,0:T(8,128)} async-done(((f32[2048,256]{1,0:T(8,128)}), f32[2048,256]{1,0:T(8,128)}) %all-reduce.7.cloned.1.call-update) | async-done | bytes 2097168 | tf_op jit(solution)/shard_map/psum | solution.py:86
  1004.2 2.7 multiply_reduce_fusion.1
  1007.0 5.5 psum.110
  1012.5 5.5 fusion.2
  1018.0 68.9 %psum.111 = f32[]{:T(128)} all-reduce(f32[]{:T(128)} %get-tuple-element.21), channel_id=1, replica_groups=mesh['pix'=64,'col'=2] {'pix','col'}, use_global_device_ids=true, to_apply=%region_11.0 | all-reduce | flops 1 | bytes 8 | tf_op jit(solution)/shard_map/psum | solution.py:91
  1088.2 7.4 fusion.3
  1095.6 64.8 %psum.112 = f32[]{:T(128)} all-reduce(f32[]{:T(128)} %get-tuple-element.5), channel_id=1, replica_groups=mesh['pix'=64,'col'=2] {'pix','col'}, use_global_device_ids=true, to_apply=%region_13.0 | all-reduce | flops 1 | bytes 8 | tf_op jit(solution)/shard_map/psum | solution.py:30
  1161.1 0.0 copy-start.3
  1161.1 2.6 multiply_subtract_fusion.2
  1163.8 1.3 copy-done
  1165.1 3.5 fusion.11
  1168.7 0.0 all-reduce.9.cloned.1.call-update
  1168.7 0.0 all-reduce.11.cloned.1.call-start
  1168.7 27.3 %all-reduce.9.cloned.1.call-done = f32[256,256]{1,0:T(8,128)} async-done(((f32[256,256]{1,0:T(8,128)}), f32[256,256]{1,0:T(8,128)}) %all-reduce.9.cloned.1.call-update) | async-done | bytes 262160 | tf_op jit(solution)/shard_map/psum | solution.py:69
  1196.0 1.6 multiply_reduce_fusion.2
  1197.6 156.7 %psum.114 = f32[]{:T(128)} all-reduce(f32[]{:T(128)} %multiply_reduce_fusion.2), channel_id=1, replica_groups=mesh['pix'=64,'col'=2] {'pix'}, use_global_device_ids=true, to_apply=%region_16.0 | all-reduce | flops 1 | bytes 8 | tf_op jit(solution)/shard_map/psum | solution.py:73
  1354.3 5.6 fusion.4
  1359.9 72.4 %psum.115 = f32[]{:T(128)} all-reduce(f32[]{:T(128)} %get-tuple-element.23), channel_id=1, replica_groups=mesh['pix'=64,'col'=2] {'pix','col'}, use_global_device_ids=true, to_apply=%region_18.0 | all-reduce | flops 1 | bytes 8 | tf_op jit(solution)/shard_map/psum | solution.py:74
  1433.8 0.0 copy-start.4
  1433.8 9.1 fusion.7
  1442.9 0.0 all-reduce.11.cloned.1.call-update
  1442.9 638.5 %all-reduce.11.cloned.1.call-done = f32[2048,256]{1,0:T(8,128)} async-done(((f32[2048,256]{1,0:T(8,128)}), f32[2048,256]{1,0:T(8,128)}) %all-reduce.11.cloned.1.call-update) | async-done | bytes 2097168 | tf_op jit(solution)/shard_map/psum | solution.py:86
  2081.4 2.7 multiply_reduce_fusion
  2084.1 5.5 psum.117
  2089.7 5.5 fusion.5
  2095.2 69.0 %psum.118 = f32[]{:T(128)} all-reduce(f32[]{:T(128)} %get-tuple-element.25), channel_id=1, replica_groups=mesh['pix'=64,'col'=2] {'pix','col'}, use_global_device_ids=true, to_apply=%region_23.0 | all-reduce | flops 1 | bytes 8 | tf_op jit(solution)/shard_map/psum | solution.py:91
  2165.4 6.5 fusion.6
  2171.9 64.7 %psum.119 = f32[]{:T(128)} all-reduce(f32[]{:T(128)} %get-tuple-element.3), channel_id=1, replica_groups=mesh['pix'=64,'col'=2] {'pix','col'}, use_global_device_ids=true, to_apply=%region_25.0 | all-reduce | flops 1 | bytes 8 | tf_op jit(solution)/shard_map/psum | solution.py:30
  2237.3 3.7 multiply_multiply_fusion.7
  2241.0 3.5 collective-permute-start.1
  2244.6 1.9 collective-permute-start
  2246.5 0.9 slice_bitcast_fusion.7
  2247.4 2.5 slice_bitcast_fusion.3
  2249.9 38.5 %collective-permute-done.1 = f32[256,2048]{1,0:T(8,128)S(1)} collective-permute-done((f32[256,2048]{1,0:T(8,128)}, f32[256,2048]{1,0:T(8,128)S(1)}, u32[]{:S(2)}, u32[]{:S(2)}) %collective-permute-start.1) | collective-permute-done | bytes 2097184 | tf_op jit(solution)/shard_map/ppermute | solution.py:18
  2288.5 4.2 collective-permute-done
  2292.7 4.4 multiply_add_fusion.1
  2297.1 3.2 collective-permute-start.3
  2300.3 1.9 collective-permute-start.2
  2302.2 0.0 copy-done.1
  2302.2 0.0 copy-done.2
  2302.3 1.6 multiply_subtract_fusion
  2303.9 0.4 slice_bitcast_fusion.1
  2304.3 39.8 %collective-permute-done.3 = f32[256,2048]{1,0:T(8,128)S(1)} collective-permute-done((f32[256,2048]{1,0:T(8,128)S(1)}, f32[256,2048]{1,0:T(8,128)S(1)}, u32[]{:S(2)}, u32[]{:S(2)}) %collective-permute-start.3) | collective-permute-done | bytes 2097184 | tf_op jit(solution)/shard_map/ppermute | solution.py:18
  2344.1 27.9 %collective-permute-done.2 = f32[256,2048]{1,0:T(8,128)S(1)} collective-permute-done((f32[256,2048]{1,0:T(8,128)S(1)}, f32[256,2048]{1,0:T(8,128)S(1)}, u32[]{:S(2)}, u32[]{:S(2)}) %collective-permute-start.2) | collective-permute-done | bytes 2097184 | tf_op jit(solution)/shard_map/ppermute | solution.py:18
  2371.9 3.3 multiply_add_fusion
  (15 shorter events, 0.1 us)
Async XLA Ops:
  7.2 111.9 %all-reduce.5.cloned.1.call-start = ((), (), s32[]{:S(2)}) async-start(), calls=%async_computation | async-start | bytes 524288 | tf_op jit(solution)/shard_map/psum | solution.py:69
  9.8 2.0 copy-start.8
  91.0 913.3 %all-reduce.7.cloned.1.call-start = ((), (), s32[]{:S(2)}) async-start(), calls=%async_computation.1 | async-start | bytes 4194304 | tf_op jit(solution)/shard_map/psum | solution.py:86
  277.5 79.3 %copy-start.6 = (f32[256,256]{1,0:T(8,128)S(1)}, f32[256,256]{1,0:T(8,128)}, u32[]{:S(2)}) copy-start(f32[256,256]{1,0:T(8,128)} %all-reduce.5.cloned.1.call-done) | copy-start | bytes 786436
  365.8 830.2 %all-reduce.9.cloned.1.call-start = ((), (), s32[]{:S(2)}) async-start(), calls=%async_computation.2 | async-start | bytes 524288 | tf_op jit(solution)/shard_map/psum | solution.py:69
  1161.1 4.0 copy-start.3
  1163.8 1.4 copy-start
  1168.7 912.7 %all-reduce.11.cloned.1.call-start = ((), (), s32[]{:S(2)}) async-start(), calls=%async_computation.3 | async-start | bytes 4194304 | tf_op jit(solution)/shard_map/psum | solution.py:86
  1354.3 79.4 %copy-start.5 = (f32[256,256]{1,0:T(8,128)S(1)}, f32[256,256]{1,0:T(8,128)}, u32[]{:S(2)}) copy-start(f32[256,256]{1,0:T(8,128)} %all-reduce.9.cloned.1.call-done) | copy-start | bytes 786436
  1433.8 655.9 %copy-start.4 = (f32[256,256]{1,0:T(8,128)}, f32[256,256]{1,0:T(8,128)S(1)}, u32[]{:S(2)}) copy-start(f32[256,256]{1,0:T(8,128)S(1)} %multiply_subtract_fusion.7) | copy-start | bytes 786436
  2241.0 47.5 %collective-permute-start.1 = (f32[256,2048]{1,0:T(8,128)}, f32[256,2048]{1,0:T(8,128)S(1)}, u32[]{:S(2)}, u32[]{:S(2)}) collective-permute-start(f32[256,2048]{1,0:T(8,128)} %multiply_multiply_fusion.7), channel_id=1, source_target_pairs={{2,0},{4,2},{6,4},{8,6},{10,8},{12,10},{14,12},{16,14},{18,16},{20... | collective-permute-start | bytes 6291464 | tf_op jit(solution)/shard_map/ppermute | solution.py:18
  2244.6 48.2 %collective-permute-start = (f32[256,2048]{1,0:T(8,128)}, f32[256,2048]{1,0:T(8,128)}, u32[]{:S(2)}, u32[]{:S(2)}) collective-permute-start(f32[256,2048]{1,0:T(8,128)} %multiply_multiply_fusion.7), channel_id=1, source_target_pairs={{0,2},{2,4},{4,6},{6,8},{8,10},{10,12},{12,14},{14,16},{16,18},{18... | collective-permute-start | bytes 6291464 | tf_op jit(solution)/shard_map/ppermute | solution.py:18
  2288.5 4.3 copy-start.7
  2292.7 9.5 copy-start.1
  2292.7 9.5 copy-start.2
  2297.1 47.0 %collective-permute-start.3 = (f32[256,2048]{1,0:T(8,128)S(1)}, f32[256,2048]{1,0:T(8,128)S(1)}, u32[]{:S(2)}, u32[]{:S(2)}) collective-permute-start(f32[256,2048]{1,0:T(8,128)S(1)} %multiply_add_fusion.1), channel_id=1, source_target_pairs={{2,0},{4,2},{6,4},{8,6},{10,8},{12,10},{14,12},{16,14},{18,16},{20... | collective-permute-start | bytes 6291464 | tf_op jit(solution)/shard_map/ppermute | solution.py:18
  2300.3 71.6 %collective-permute-start.2 = (f32[256,2048]{1,0:T(8,128)S(1)}, f32[256,2048]{1,0:T(8,128)S(1)}, u32[]{:S(2)}, u32[]{:S(2)}) collective-permute-start(f32[256,2048]{1,0:T(8,128)S(1)} %multiply_add_fusion.1), channel_id=1, source_target_pairs={{0,2},{2,4},{4,6},{6,8},{8,10},{10,12},{12,14},{14,16},{16,18},{18... | collective-permute-start | bytes 6291464 | tf_op jit(solution)/shard_map/ppermute | solution.py:18
Sparse Core Ops, SparseCore 0:
  91.1 27.9 all-reduce.4
  366.0 638.2 all-reduce.6
  1168.8 27.1 all-reduce.8
  1443.0 638.2 all-reduce.10
where the time goes:
time: 2390 us; the launch traced here: 2380 us
  waiting for transfers between devices  1440 us (60%)
  blocking collectives  803 us (34%)
  matrix products  56.5 us (2%)
  other arithmetic  39.3 us (2%)
    psum x2, waiting for transfers between devices, per_device(): col_grad = lax.psum(local_grad, 'pix')  1280 us
    psum x2, blocking collectives, per_device(): top_sum = lax.psum(norm_local, 'pix')  313 us
    psum x4, blocking collectives, per_device(): bottom_sum = lax.psum(curve_local, ('pix', 'col'))  283 us
    psum x3, blocking collectives, level_of(): spread = lax.psum(jnp.sum(weight * residual * residual), ('pix', 'col'))  195 us
    ppermute x4, waiting for transfers between devices, passed_along(): return lax.ppermute(block, axis, route)  110 us
    psum x2, waiting for transfers between devices, per_device(): pix_grad = lax.psum(jnp.dot(misfit, col_fac, precision=highest), 'col')  55.3 us
  transfers between devices with their start and end apart: 8, of which 8 were waited for; matrix products, arithmetic and copies ran while one was open for 0% of the time, Pallas kernels for 0%

commit v1 on v0

--- a/solution.py
+++ b/solution.py
@@ -1,3 +1,4 @@
+import functools
 import jax
 import jax.numpy as jnp
 from jax import lax
@@ -10,6 +11,13 @@
 highest = lax.Precision.HIGHEST
 threshold_scale = 1.0
 diffusion = 0.2
+
+
+def follow_view(view, dev_axis, shard_axis):
+    return lax.psum(lax.psum(view, axis_name=dev_axis), axis_name=shard_axis)
+
+
+plan_threads = functools.partial(follow_view, dev_axis="pix", shard_axis="col")
 
 
 def passed_along(block, axis, distance):
@@ -71,7 +79,7 @@
         norm_local = jnp.sum(pix_grad * pix_grad)
         curve_local = jnp.sum(weight * change * change)
         top_sum = lax.psum(norm_local, "pix")
-        bottom_sum = lax.psum(curve_local, ("pix", "col"))
+        bottom_sum = plan_threads(curve_local)
         step_pix = top_sum / bottom_sum
         pix_fac = pix_fac - step_pix * pix_grad
         low_rank = low_rank - step_pix * change

time: 2390 us -> 2270 us (0.950)
  blocking collectives: 803 us -> 669 us
    psum x4 -> x2, blocking collectives: 283 us -> 138 us  [per_device(): bottom_sum = lax.psum(curve_local, ('pix', 'col'))]
where the time goes in v1:
time: 2270 us; the launch traced here: 2260 us
  waiting for transfers between devices  1460 us (64%)
  blocking collectives  669 us (29%)
  matrix products  56.5 us (2%)
  other arithmetic  39.3 us (2%)
    psum x2, waiting for transfers between devices, per_device(): col_grad = lax.psum(local_grad, 'pix')  1290 us
    psum x2, blocking collectives, per_device(): top_sum = lax.psum(norm_local, 'pix')  314 us
    psum x3, blocking collectives, level_of(): spread = lax.psum(jnp.sum(weight * residual * residual), ('pix', 'col'))  195 us
    psum x2, blocking collectives, per_device(): bottom_sum = lax.psum(curve_local, ('pix', 'col'))  138 us
    ppermute x4, waiting for transfers between devices, passed_along(): return lax.ppermute(block, axis, route)  110 us
    psum x2, waiting for transfers between devices, per_device(): pix_grad = lax.psum(jnp.dot(misfit, col_fac, precision=highest), 'col')  55.3 us
  transfers between devices with their start and end apart: 8, of which 8 were waited for; matrix products, arithmetic and copies ran while one was open for 0% of the time, Pallas kernels for 0%

profile of v1, /device:TPU:32, one launch (start us, length us, event | category | flops | bytes accessed | tf_op | source)
XLA Modules:
  0.0 2262.6 jit_solution(14642473538224171193)
XLA Ops:
  7.2 0.0 all-reduce.7.cloned.1.call-start
  7.2 1.0 convert_element_type.3
  8.2 0.1 copy.7
  8.3 1.5 broadcast_bitcast_fusion
  9.8 2.0 copy.10
  11.8 0.0 copy-done.8
  11.8 7.0 fusion
  18.7 65.8 %psum.119 = f32[]{:T(128)} all-reduce(f32[]{:T(128)} %get-tuple-element.12), channel_id=1, replica_groups=mesh['pix'=64,'col'=2] {'pix','col'}, use_global_device_ids=true, to_apply=%region_1.0 | all-reduce | flops 1 | bytes 8 | tf_op jit(solution)/shard_map/psum | solution.py:38
  85.2 5.7 fusion.20
  91.0 0.0 all-reduce.7.cloned.1.call-update
  91.0 0.0 all-reduce.9.cloned.1.call-start
  91.0 28.1 %all-reduce.7.cloned.1.call-done = f32[256,256]{1,0:T(8,128)} async-done(((f32[256,256]{1,0:T(8,128)}), f32[256,256]{1,0:T(8,128)}) %all-reduce.7.cloned.1.call-update) | async-done | bytes 262160 | tf_op jit(solution)/shard_map/psum | solution.py:77
  119.1 1.6 multiply_reduce_fusion.3
  120.7 5.6 fusion.1
  126.4 156.7 %all-reduce.1 = (f32[]{:T(128)}, f32[]{:T(128)}) all-reduce(f32[]{:T(128)} %multiply_reduce_fusion.3, f32[]{:T(128)} %get-tuple-element.23), channel_id=1, replica_groups=mesh['pix'=64,'col'=2] {'pix'}, use_global_device_ids=true, to_apply=%region_4.0 | all-reduce | flops 2 | bytes 16 | tf_op jit(solution)/shard_map/psum | solution.py:81
  283.1 6.0 psum.123
  290.4 9.0 fusion.16
  299.4 0.0 all-reduce.9.cloned.1.call-update
  299.4 0.0 all-reduce.11.cloned.1.call-start
  299.5 645.4 %all-reduce.9.cloned.1.call-done = f32[2048,256]{1,0:T(8,128)} async-done(((f32[2048,256]{1,0:T(8,128)}), f32[2048,256]{1,0:T(8,128)}) %all-reduce.9.cloned.1.call-update) | async-done | bytes 2097168 | tf_op jit(solution)/shard_map/psum | solution.py:94
  944.9 2.7 multiply_reduce_fusion.1
  947.6 5.5 psum.125
  953.1 5.5 fusion.2
  958.6 68.9 %psum.126 = f32[]{:T(128)} all-reduce(f32[]{:T(128)} %get-tuple-element.25), channel_id=1, replica_groups=mesh['pix'=64,'col'=2] {'pix','col'}, use_global_device_ids=true, to_apply=%region_12.0 | all-reduce | flops 1 | bytes 8 | tf_op jit(solution)/shard_map/psum | solution.py:99
  1028.8 7.4 fusion.3
  1036.3 64.7 %psum.127 = f32[]{:T(128)} all-reduce(f32[]{:T(128)} %get-tuple-element.9), channel_id=1, replica_groups=mesh['pix'=64,'col'=2] {'pix','col'}, use_global_device_ids=true, to_apply=%region_14.0 | all-reduce | flops 1 | bytes 8 | tf_op jit(solution)/shard_map/psum | solution.py:38
  1101.7 0.0 copy-start.3
  1101.7 2.6 multiply_subtract_fusion.2
  1104.4 1.3 copy-done
  1105.7 3.5 fusion.11
  1109.3 0.0 all-reduce.11.cloned.1.call-update
  1109.3 0.0 all-reduce.13.cloned.1.call-start
  1109.3 27.3 %all-reduce.11.cloned.1.call-done = f32[256,256]{1,0:T(8,128)} async-done(((f32[256,256]{1,0:T(8,128)}), f32[256,256]{1,0:T(8,128)}) %all-reduce.11.cloned.1.call-update) | async-done | bytes 262160 | tf_op jit(solution)/shard_map/psum | solution.py:77
  1136.6 1.6 multiply_reduce_fusion.2
  1138.2 5.6 fusion.4
  1143.8 156.8 %all-reduce = (f32[]{:T(128)}, f32[]{:T(128)}) all-reduce(f32[]{:T(128)} %multiply_reduce_fusion.2, f32[]{:T(128)} %get-tuple-element.27), channel_id=1, replica_groups=mesh['pix'=64,'col'=2] {'pix'}, use_global_device_ids=true, to_apply=%region_17.0 | all-reduce | flops 2 | bytes 16 | tf_op jit(solution)/shard_map/psum | solution.py:81
  1300.6 5.5 psum.131
  1307.5 0.0 copy-start.4
  1307.5 9.1 fusion.7
  1316.6 0.0 all-reduce.13.cloned.1.call-update
  1316.6 645.5 %all-reduce.13.cloned.1.call-done = f32[2048,256]{1,0:T(8,128)} async-done(((f32[2048,256]{1,0:T(8,128)}), f32[2048,256]{1,0:T(8,128)}) %all-reduce.13.cloned.1.call-update) | async-done | bytes 2097168 | tf_op jit(solution)/shard_map/psum | solution.py:94
  1962.1 2.7 multiply_reduce_fusion
  1964.8 5.8 psum.133
  1970.6 5.5 fusion.5
  1976.1 69.0 %psum.134 = f32[]{:T(128)} all-reduce(f32[]{:T(128)} %get-tuple-element.29), channel_id=1, replica_groups=mesh['pix'=64,'col'=2] {'pix','col'}, use_global_device_ids=true, to_apply=%region_25.0 | all-reduce | flops 1 | bytes 8 | tf_op jit(solution)/shard_map/psum | solution.py:99
  2046.3 6.5 fusion.6
  2052.8 64.4 %psum.135 = f32[]{:T(128)} all-reduce(f32[]{:T(128)} %get-tuple-element.7), channel_id=1, replica_groups=mesh['pix'=64,'col'=2] {'pix','col'}, use_global_device_ids=true, to_apply=%region_27.0 | all-reduce | flops 1 | bytes 8 | tf_op jit(solution)/shard_map/psum | solution.py:38
  2117.9 3.7 multiply_multiply_fusion.7
  2121.6 3.5 collective-permute-start.1
  2125.2 1.9 collective-permute-start
  2127.1 0.9 slice_bitcast_fusion.7
  2128.0 2.5 slice_bitcast_fusion.3
  2130.5 38.5 %collective-permute-done.1 = f32[256,2048]{1,0:T(8,128)S(1)} collective-permute-done((f32[256,2048]{1,0:T(8,128)}, f32[256,2048]{1,0:T(8,128)S(1)}, u32[]{:S(2)}, u32[]{:S(2)}) %collective-permute-start.1) | collective-permute-done | bytes 2097184 | tf_op jit(solution)/shard_map/ppermute | solution.py:26
  2169.1 4.2 collective-permute-done
  2173.3 4.4 multiply_add_fusion.1
  2177.7 3.2 collective-permute-start.3
  2180.9 1.9 collective-permute-start.2
  2182.8 0.0 copy-done.1
  2182.8 0.0 copy-done.2
  2182.9 1.6 multiply_subtract_fusion
  2184.5 0.4 slice_bitcast_fusion.1
  2184.9 39.8 %collective-permute-done.3 = f32[256,2048]{1,0:T(8,128)S(1)} collective-permute-done((f32[256,2048]{1,0:T(8,128)S(1)}, f32[256,2048]{1,0:T(8,128)S(1)}, u32[]{:S(2)}, u32[]{:S(2)}) %collective-permute-start.3) | collective-permute-done | bytes 2097184 | tf_op jit(solution)/shard_map/ppermute | solution.py:26
  2224.7 27.9 %collective-permute-done.2 = f32[256,2048]{1,0:T(8,128)S(1)} collective-permute-done((f32[256,2048]{1,0:T(8,128)S(1)}, f32[256,2048]{1,0:T(8,128)S(1)}, u32[]{:S(2)}, u32[]{:S(2)}) %collective-permute-start.2) | collective-permute-done | bytes 2097184 | tf_op jit(solution)/shard_map/ppermute | solution.py:26
  2252.5 3.3 multiply_add_fusion
  (15 shorter events, 0.1 us)
Async XLA Ops:
  7.2 111.9 %all-reduce.7.cloned.1.call-start = ((), (), s32[]{:S(2)}) async-start(), calls=%async_computation | async-start | bytes 524288 | tf_op jit(solution)/shard_map/psum | solution.py:77
  9.8 2.0 copy-start.8
  91.0 853.9 %all-reduce.9.cloned.1.call-start = ((), (), s32[]{:S(2)}) async-start(), calls=%async_computation.1 | async-start | bytes 4194304 | tf_op jit(solution)/shard_map/psum | solution.py:94
  120.7 169.6 %copy-start.6 = (f32[256,256]{1,0:T(8,128)S(1)}, f32[256,256]{1,0:T(8,128)}, u32[]{:S(2)}) copy-start(f32[256,256]{1,0:T(8,128)} %all-reduce.7.cloned.1.call-done) | copy-start | bytes 786436
  299.4 837.2 %all-reduce.11.cloned.1.call-start = ((), (), s32[]{:S(2)}) async-start(), calls=%async_computation.2 | async-start | bytes 524288 | tf_op jit(solution)/shard_map/psum | solution.py:77
  1101.7 4.0 copy-start.3
  1104.4 1.4 copy-start
  1109.3 852.8 %all-reduce.13.cloned.1.call-start = ((), (), s32[]{:S(2)}) async-start(), calls=%async_computation.3 | async-start | bytes 4194304 | tf_op jit(solution)/shard_map/psum | solution.py:94
  1138.2 169.2 %copy-start.5 = (f32[256,256]{1,0:T(8,128)S(1)}, f32[256,256]{1,0:T(8,128)}, u32[]{:S(2)}) copy-start(f32[256,256]{1,0:T(8,128)} %all-reduce.11.cloned.1.call-done) | copy-start | bytes 786436
  1307.5 663.1 %copy-start.4 = (f32[256,256]{1,0:T(8,128)}, f32[256,256]{1,0:T(8,128)S(1)}, u32[]{:S(2)}) copy-start(f32[256,256]{1,0:T(8,128)S(1)} %multiply_subtract_fusion.7) | copy-start | bytes 786436
  2121.6 47.5 %collective-permute-start.1 = (f32[256,2048]{1,0:T(8,128)}, f32[256,2048]{1,0:T(8,128)S(1)}, u32[]{:S(2)}, u32[]{:S(2)}) collective-permute-start(f32[256,2048]{1,0:T(8,128)} %multiply_multiply_fusion.7), channel_id=1, source_target_pairs={{2,0},{4,2},{6,4},{8,6},{10,8},{12,10},{14,12},{16,14},{18,16},{20... | collective-permute-start | bytes 6291464 | tf_op jit(solution)/shard_map/ppermute | solution.py:26
  2125.2 48.2 %collective-permute-start = (f32[256,2048]{1,0:T(8,128)}, f32[256,2048]{1,0:T(8,128)}, u32[]{:S(2)}, u32[]{:S(2)}) collective-permute-start(f32[256,2048]{1,0:T(8,128)} %multiply_multiply_fusion.7), channel_id=1, source_target_pairs={{0,2},{2,4},{4,6},{6,8},{8,10},{10,12},{12,14},{14,16},{16,18},{18... | collective-permute-start | bytes 6291464 | tf_op jit(solution)/shard_map/ppermute | solution.py:26
  2169.1 4.3 copy-start.7
  2173.3 9.5 copy-start.1
  2173.3 9.5 copy-start.2
  2177.7 47.0 %collective-permute-start.3 = (f32[256,2048]{1,0:T(8,128)S(1)}, f32[256,2048]{1,0:T(8,128)S(1)}, u32[]{:S(2)}, u32[]{:S(2)}) collective-permute-start(f32[256,2048]{1,0:T(8,128)S(1)} %multiply_add_fusion.1), channel_id=1, source_target_pairs={{2,0},{4,2},{6,4},{8,6},{10,8},{12,10},{14,12},{16,14},{18,16},{20... | collective-permute-start | bytes 6291464 | tf_op jit(solution)/shard_map/ppermute | solution.py:26
  2180.9 71.6 %collective-permute-start.2 = (f32[256,2048]{1,0:T(8,128)S(1)}, f32[256,2048]{1,0:T(8,128)S(1)}, u32[]{:S(2)}, u32[]{:S(2)}) collective-permute-start(f32[256,2048]{1,0:T(8,128)S(1)} %multiply_add_fusion.1), channel_id=1, source_target_pairs={{0,2},{2,4},{4,6},{6,8},{8,10},{10,12},{12,14},{14,16},{16,18},{18... | collective-permute-start | bytes 6291464 | tf_op jit(solution)/shard_map/ppermute | solution.py:26
Sparse Core Ops, SparseCore 0:
  91.1 27.9 all-reduce.6
  299.5 645.2 all-reduce.8
  1109.4 27.1 all-reduce.10
  1316.7 645.2 all-reduce.12
